TPU v7x, 128 devices: a whole 4x4x4 slice. The times are simulated.
128 devices in a mesh: tok: 4 (over z_lo, core), con: 4 (over x), out: 8 (over z_hi, y).
Axes of the slice: x: 4, y: 4, z: 4 (z_hi: 2, z_lo: 2; z = z_hi * 2 + z_lo), core: 2. Of those that a mesh axis runs over, the one named last changes fastest.
Arguments:
- tokens: bfloat16 [1024, 10240], P('tok', 'con'), may hold values from -6 to 6
- out_grad: bfloat16 [1024, 10240], P('tok', 'con'), may hold values from -3 to 3
- weight_in: bfloat16 [10240, 20480], P('con', ('tok', 'out')), may hold values from -0.0625 to 0.0625
- weight_out: bfloat16 [20480, 10240], P(('tok', 'out'), 'con'), may hold values from -0.0390625 to 0.0390625
Outputs:
- input_grad: bfloat16 [1024, 10240], P(('tok', 'out'), 'con')
- first_grad: float32 [10240, 20480], P('con', ('tok', 'out'))
- second_grad: float32 [20480, 10240], P(('tok', 'out'), 'con')
All inputs are finite; a program needn't handle non-finite values.
Results may differ from a plain program's by a relative error of at most 0.0049.
Values may be sent and summed in bfloat16 or wider, within the bound.
No kernel may reach another device: no remote copies, remote signals or barrier semaphores. Data moves between devices by JAX's collectives and lax.ppermute only.
A program may use at most 128 MiB of HBM per device.

v0:
```python
import jax
import jax.numpy as jnp
from jax import lax
from jax.sharding import PartitionSpec as P


def gelu_parts(pre, act_grad):
    cdf = 0.5 * (1.0 + jax.scipy.special.erf(pre * 0.7071067811865476))
    density = jnp.exp(-0.5 * pre * pre) * 0.3989422804014327
    activ = (pre * cdf).astype(jnp.bfloat16)
    pre_grad = (act_grad * (cdf + pre * density)).astype(jnp.bfloat16)
    return (activ, pre_grad)


def per_device(tokens, out_grad, weight_in, weight_out):
    gathered_tok, gathered_grad = (
        lax.all_gather(tokens, "tok", axis=0, tiled=True),
        lax.all_gather(out_grad, "tok", axis=0, tiled=True),
    )
    pre_part = jnp.dot(gathered_tok, weight_in, preferred_element_type=jnp.float32)
    grad_part = lax.dot_general(
        gathered_grad, weight_out, (((1,), (1,)), ((), ())), preferred_element_type=jnp.float32
    )
    pre, act_grad = lax.psum((pre_part, grad_part), "con")
    activ, pre_grad = gelu_parts(pre, act_grad)
    first_grad = lax.dot_general(
        gathered_tok, pre_grad, (((0,), (0,)), ((), ())), preferred_element_type=jnp.float32
    )
    second_grad = lax.dot_general(
        activ, gathered_grad, (((0,), (0,)), ((), ())), preferred_element_type=jnp.float32
    )
    summed = lax.psum_scatter(
        lax.dot_general(
            pre_grad, weight_in, (((1,), (1,)), ((), ())), preferred_element_type=jnp.float32
        ),
        ("tok", "out"),
        scatter_dimension=0,
        tiled=True,
    )
    return (summed.astype(jnp.bfloat16), first_grad, second_grad)


def solution(mesh):
    placed = (P("tok", "con"), P("tok", "con"), P("con", ("tok", "out")), P(("tok", "out"), "con"))
    return jax.shard_map(
        per_device,
        mesh=mesh,
        in_specs=placed,
        out_specs=(P(("tok", "out"), "con"), P("con", ("tok", "out")), P(("tok", "out"), "con")),
        check_vma=False,
    )
```

profile of v0, /device:TPU:26, one launch (start us, length us, event | category | flops | bytes accessed | tf_op | source)
XLA Modules:
  0.0 438.6 jit_solution(11786640155277822944)
XLA Ops:
  7.2 0.0 copy-start
  7.2 0.0 all-gather.3.cloned.1.call-start
  7.2 0.7 all-gather.3.cloned.1.call-update
  7.9 0.0 all-gather.5.cloned.1.call-start
  8.0 0.7 all-gather.5.cloned.1.call-update
  8.7 0.0 all-reduce.3.cloned.1.call-start
  8.7 57.5 %all-gather.3.cloned.1.call-done = bf16[1024,2560]{1,0:T(8,128)(2,1)} async-done(((bf16[256,2560]{1,0:T(8,128)(2,1)}), bf16[1024,2560]{1,0:T(8,128)(2,1)}) %all-gather.3.cloned.1.call-update) | async-done | bytes 5242896 | tf_op jit(solution)/shard_map/all_gather | solution.py:18
  66.2 9.2 %fusion.7 = f32[1024,640]{1,0:T(8,128)} fusion(bf16[1024,2560]{1,0:T(8,128)(2,1)} %all-gather.3.cloned.1.call-done, bf16[640,2560]{1,0:T(8,128)(2,1)} %param.7), kind=kOutput, calls=%fused_computation.11 | convolution fusion | flops 3355443200 | bytes 11141120 | tf_op jit(solution)/shard_map/dot_general | solution.py:21
  75.4 48.6 %all-gather.5.cloned.1.call-done = bf16[1024,2560]{1,0:T(8,128)(2,1)} async-done(((bf16[256,2560]{1,0:T(8,128)(2,1)}), bf16[1024,2560]{1,0:T(8,128)(2,1)}) %all-gather.5.cloned.1.call-update) | async-done | bytes 5242896 | tf_op jit(solution)/shard_map/all_gather | solution.py:17
  124.0 0.0 copy-done
  124.0 8.2 %fusion.8 = f32[1024,640]{1,0:T(8,128)} fusion(bf16[1024,2560]{1,0:T(8,128)(2,1)} %all-gather.5.cloned.1.call-done, bf16[2560,640]{1,0:T(8,128)(2,1)S(1)} %copy-done), kind=kOutput, calls=%fused_computation.12 | convolution fusion | flops 3355443200 | bytes 11141120 | tf_op jit(solution)/shard_map/dot_general | solution.py:20
  132.2 0.0 all-reduce.3.cloned.1.call-update
  132.3 0.2 reduce-scatter.2.cloned.1.call-start
  132.5 110.4 %all-reduce.3.cloned.1.call-done = (f32[1024,640]{1,0:T(8,128)}, f32[1024,640]{1,0:T(8,128)}) async-done(((f32[1024,640]{1,0:T(8,128)}, f32[1024,640]{1,0:T(8,128)}), (f32[1024,640]{1,0:T(8,128)}, f32[1024,640]{1,0:T(8,128)})) %all-reduce.3.cloned.1.call-update) | async-done | bytes 5242896 | tf_op jit(solution)/shard_map/psum | solution.py:24
  242.9 3.1 fusion.5
  245.9 0.0 copy-start.1
  246.0 1.0 copy-done.1
  247.0 6.9 %fusion.9 = f32[1024,2560]{1,0:T(8,128)} fusion(bf16[1024,640]{1,0:T(8,128)(2,1)S(1)} %fusion.5, bf16[2560,640]{1,0:T(8,128)(2,1)S(1)} %copy-done), kind=kOutput, calls=%fused_computation.13 | convolution fusion | flops 3355443200 | bytes 15073280 | tf_op jit(solution)/shard_map/dot_general | solution.py:33
  253.9 0.0 reduce-scatter.2.cloned.1.call-update
  254.0 9.3 %convolution_bitcast_fusion = f32[2560,640]{0,1:T(8,128)} fusion(bf16[1024,640]{1,0:T(8,128)(2,1)} %copy-done.1, bf16[1024,2560]{1,0:T(8,128)(2,1)} %all-gather.5.cloned.1.call-done), kind=kOutput, calls=%fused_computation | convolution fusion | flops 3355443200 | bytes 13107200 | tf_op jit(solution)/shard_map/dot_general | solution.py:26
  263.2 8.3 %copy.7 = f32[2560,640]{1,0:T(8,128)} copy(f32[2560,640]{0,1:T(8,128)} %convolution_bitcast_fusion) | data formatting | bytes 13107200
  271.5 9.7 %fusion.6 = f32[640,2560]{1,0:T(8,128)} fusion(bf16[1024,2560]{1,0:T(8,128)(2,1)} %all-gather.3.cloned.1.call-done, f32[1024,640]{1,0:T(8,128)} %get-tuple-element.7), kind=kOutput, calls=%fused_computation.10 | convolution fusion | flops 3358720000 | bytes 14417920 | tf_op jit(solution)/shard_map/dot_general | solution.py:29
  281.2 149.2 %reduce-scatter.2.cloned.1.call-done = f32[32,2560]{1,0:T(8,128)} async-done(((f32[1024,2560]{1,0:T(8,128)}), f32[32,2560]{1,0:T(8,128)}) %reduce-scatter.2.cloned.1.call-update) | async-done | bytes 327696 | tf_op jit(solution)/shard_map/reduce_scatter | solution.py:32
  430.4 1.7 convert_element_type.10
Async XLA Ops:
  7.2 116.9 %copy-start = (bf16[2560,640]{1,0:T(8,128)(2,1)S(1)}, bf16[2560,640]{1,0:T(8,128)(2,1)}, u32[]{:S(2)}) copy-start(bf16[2560,640]{1,0:T(8,128)(2,1)} %param.6) | copy-start | bytes 9830404
  7.2 59.0 %all-gather.3.cloned.1.call-start = ((), (), s32[]{:S(2)}) async-start(), calls=%async_computation.1 | async-start | bytes 6553600 | tf_op jit(solution)/shard_map/all_gather | solution.py:18
  7.9 116.1 %all-gather.5.cloned.1.call-start = ((), (), s32[]{:S(2)}) async-start(), calls=%async_computation.2 | async-start | bytes 6553600 | tf_op jit(solution)/shard_map/all_gather | solution.py:17
  8.7 234.2 %all-reduce.3.cloned.1.call-start = ((), (), s32[]{:S(2)}) async-start(), calls=%async_computation.4 | async-start | bytes 10485760 | tf_op jit(solution)/shard_map/psum | solution.py:24
  132.3 298.1 %reduce-scatter.2.cloned.1.call-start = ((), (), s32[]{:S(2)}) async-start(), calls=%async_computation.3 | async-start | bytes 10813440 | tf_op jit(solution)/shard_map/reduce_scatter | solution.py:32
  245.9 1.1 copy-start.1
Sparse Core Ops, SparseCore 0:
  9.6 56.4 all-gather.2
  67.8 56.1 all-gather.4
  132.4 110.4 all-reduce.2
  254.1 176.2 reduce-scatter.1
where the time goes:
time: 439 us
  waiting for transfers between devices  367 us (84%)
  matrix products  43.4 us (10%)
  between operations  13.8 us (3%)
  local copies, waits for them, and re-layouts  9.32 us (2%)
  other arithmetic  4.71 us (1%)
    reduce_scatter x1, waiting for transfers between devices, per_device(): lax.psum_scatter(lax.dot_general(pre_grad, weight_in, (((1,), (1,)), ((),...  149 us
    psum x1, waiting for transfers between devices, per_device(): pre, act_grad = lax.psum((pre_part, grad_part), 'con')  110 us
    all_gather x1, waiting for transfers between devices, per_device(): lax.all_gather(out_grad, 'tok', axis=0, tiled=True)  57.5 us
    all_gather x1, waiting for transfers between devices, per_device(): lax.all_gather(tokens, 'tok', axis=0, tiled=True)  48.6 us
    dot_general x1, matrix products, per_device(): lax.dot_general(activ, gathered_grad, (((0,), (0,)), ((), ())), preferred...  9.72 us
    unnamed x5, local copies, waits for them, and re-layouts  9.32 us
    dot_general x1, matrix products, per_device(): lax.dot_general(gathered_tok, pre_grad, (((0,), (0,)), ((), ())), preferr...  9.29 us
    dot_general x1, matrix products, per_device(): lax.dot_general(gathered_grad, weight_out, (((1,), (1,)), ((), ())), pref...  9.24 us
  transfers between devices with their start and end apart: 4, of which 4 were waited for; matrix products, arithmetic and copies ran while one was open for 8% of the time, Pallas kernels for 0%

commit v1 on v0

--- a/solution.py
+++ b/solution.py
@@ -2,6 +2,13 @@
 import jax.numpy as jnp
 from jax import lax
 from jax.sharding import PartitionSpec as P
+from jax.lax import all_to_all, axis_size
+
+
+def edit_points(inputs):
+    far_arr = jnp.stack([inputs] * axis_size("tok"), axis=0)
+    v_next = all_to_all(far_arr, "tok", 0, 0)
+    return jnp.concatenate(v_next, 0)
 
 
 def gelu_parts(pre, act_grad):
@@ -14,7 +21,7 @@
 
 def per_device(tokens, out_grad, weight_in, weight_out):
     gathered_tok, gathered_grad = (
-        lax.all_gather(tokens, "tok", axis=0, tiled=True),
+        edit_points(tokens),
         lax.all_gather(out_grad, "tok", axis=0, tiled=True),
     )
     pre_part = jnp.dot(gathered_tok, weight_in, preferred_element_type=jnp.float32)

time: 439 us -> 438 us (level)
  waiting for transfers between devices: 367 us -> 258 us
  blocking collectives: 0 us -> 104 us
  local copies, waits for them, and re-layouts: 9.32 us -> 14.8 us
    all_to_all x0 -> x1, blocking collectives: none -> 104 us  [edit_points(): v_next = all_to_all(far_arr, 'tok', 0, 0)]
    all_gather x1, waiting for transfers between devices: 57.5 us -> 0.01 us  [per_device(): lax.all_gather(out_grad, 'tok', axis=0, tiled=True)]
    all_gather x1 -> x0, waiting for transfers between devices: 48.6 us -> none  [per_device(): lax.all_gather(tokens, 'tok', axis=0, tiled=True)]
    unnamed x5 -> x11, local copies, waits for them, and re-layouts: 9.32 us -> 12.9 us
  transfers between devices with their start and end apart: 4 -> 3, of which waited for: 4 -> 2; matrix products, arithmetic and copies ran while one was open for 8% -> 8% of each run, Pallas kernels for 0% -> 0%
where the time goes in v1:
time: 438 us; the launch traced here: 436 us
  waiting for transfers between devices  258 us (59%)
  blocking collectives  104 us (24%)
  matrix products  40.7 us (9%)
  local copies, waits for them, and re-layouts  14.8 us (3%)
  between operations  13.8 us (3%)
  other arithmetic  4.71 us (1%)
    reduce_scatter x1, waiting for transfers between devices, per_device(): lax.psum_scatter(lax.dot_general(pre_grad, weight_in, (((1,), (1,)), ((),...  147 us
    psum x1, waiting for transfers between devices, per_device(): pre, act_grad = lax.psum((pre_part, grad_part), 'con')  110 us
    all_to_all x1, blocking collectives, edit_points(): v_next = all_to_all(far_arr, 'tok', 0, 0)  104 us
    unnamed x11, local copies, waits for them, and re-layouts  12.9 us
    dot_general x1, matrix products, per_device(): lax.dot_general(activ, gathered_grad, (((0,), (0,)), ((), ())), preferred...  9.87 us
    dot_general x1, matrix products, per_device(): lax.dot_general(gathered_grad, weight_out, (((1,), (1,)), ((), ())), pref...  9.24 us
    dot_general x1, matrix products, per_device(): lax.dot_general(gathered_tok, pre_grad, (((0,), (0,)), ((), ())), preferr...  8.88 us
  transfers between devices with their start and end apart: 3, of which 2 were waited for; matrix products, arithmetic and copies ran while one was open for 8% of the time, Pallas kernels for 0%

profile of v1, /device:TPU:26, one launch (start us, length us, event | category | flops | bytes accessed | tf_op | source)
XLA Modules:
  0.0 436.3 jit_solution(2214214561377529420)
XLA Ops:
  7.2 0.0 copy-start
  7.2 0.0 all-gather.2.cloned.1.call-start
  7.2 0.7 all-gather.2.cloned.1.call-update
  7.9 0.0 all-reduce.3.cloned.1.call-start
  8.0 1.9 stack.2
  9.9 104.5 %all_to_all.5 = bf16[4,256,2560]{2,1,0:T(8,128)(2,1)S(1)} all-to-all(bf16[4,256,2560]{2,1,0:T(8,128)(2,1)S(1)} %stack.2), channel_id=1, replica_groups=mesh['tok'=4,'con'=4,'out'=8] {'tok'}, dimensions={0} | all-to-all | bytes 10485760 | tf_op jit(solution)/shard_map/all_to_all | solution.py:10
  114.4 0.0 copy-start.2
  114.4 2.4 copy-done.2
  116.7 0.0 copy-done
  116.7 5.8 %fusion.8 = f32[1024,640]{1,0:T(8,128)} fusion(bf16[1024,2560]{1,0:T(8,128)(2,1)S(1)} %bitcast.12, bf16[2560,640]{1,0:T(8,128)(2,1)S(1)} %copy-done), kind=kOutput, calls=%fused_computation.12 | convolution fusion | flops 3355443200 | bytes 11141120 | tf_op jit(solution)/shard_map/dot_general | solution.py:27
  122.5 0.0 all-gather.2.cloned.1.call-done
  122.5 9.2 %fusion.7 = f32[1024,640]{1,0:T(8,128)} fusion(bf16[1024,2560]{1,0:T(8,128)(2,1)} %all-gather.2.cloned.1.call-done, bf16[640,2560]{1,0:T(8,128)(2,1)} %param.7), kind=kOutput, calls=%fused_computation.11 | convolution fusion | flops 3355443200 | bytes 11141120 | tf_op jit(solution)/shard_map/dot_general | solution.py:28
  131.7 0.0 all-reduce.3.cloned.1.call-update
  131.8 0.2 reduce-scatter.2.cloned.1.call-start
  132.0 110.3 %all-reduce.3.cloned.1.call-done = (f32[1024,640]{1,0:T(8,128)}, f32[1024,640]{1,0:T(8,128)}) async-done(((f32[1024,640]{1,0:T(8,128)}, f32[1024,640]{1,0:T(8,128)}), (f32[1024,640]{1,0:T(8,128)}, f32[1024,640]{1,0:T(8,128)})) %all-reduce.3.cloned.1.call-update) | async-done | bytes 5242896 | tf_op jit(solution)/shard_map/psum | solution.py:31
  242.2 3.1 fusion.5
  245.3 0.0 copy-start.3
  245.3 1.0 copy-done.3
  246.4 6.9 %fusion.9 = f32[1024,2560]{1,0:T(8,128)} fusion(bf16[1024,640]{1,0:T(8,128)(2,1)S(1)} %fusion.5, bf16[2560,640]{1,0:T(8,128)(2,1)S(1)} %copy-done), kind=kOutput, calls=%fused_computation.13 | convolution fusion | flops 3355443200 | bytes 15073280 | tf_op jit(solution)/shard_map/dot_general | solution.py:40
  253.3 0.0 copy-start.4
  253.3 0.0 reduce-scatter.2.cloned.1.call-update
  253.3 1.3 copy-done.4
  254.6 8.9 %convolution_bitcast_fusion = f32[2560,640]{0,1:T(8,128)} fusion(bf16[1024,640]{1,0:T(8,128)(2,1)S(1)} %copy-done.4, bf16[1024,2560]{1,0:T(8,128)(2,1)} %bitcast.13), kind=kOutput, calls=%fused_computation | convolution fusion | flops 3355443200 | bytes 13107200 | tf_op jit(solution)/shard_map/dot_general | solution.py:33
  263.5 8.1 %copy.7 = f32[2560,640]{1,0:T(8,128)} copy(f32[2560,640]{0,1:T(8,128)} %convolution_bitcast_fusion) | data formatting | bytes 13107200
  271.6 0.0 copy-start.1
  271.6 9.9 %fusion.6 = f32[640,2560]{1,0:T(8,128)} fusion(bf16[1024,2560]{1,0:T(8,128)(2,1)} %all-gather.2.cloned.1.call-done, f32[1024,640]{1,0:T(8,128)} %get-tuple-element.7), kind=kOutput, calls=%fused_computation.10 | convolution fusion | flops 3358720000 | bytes 14417920 | tf_op jit(solution)/shard_map/dot_general | solution.py:36
  281.5 146.7 %reduce-scatter.2.cloned.1.call-done = f32[32,2560]{1,0:T(8,128)} async-done(((f32[1024,2560]{1,0:T(8,128)}), f32[32,2560]{1,0:T(8,128)}) %reduce-scatter.2.cloned.1.call-update) | async-done | bytes 327696 | tf_op jit(solution)/shard_map/reduce_scatter | solution.py:39
  428.2 1.7 convert_element_type.10
  429.8 0.0 copy-done.1
Async XLA Ops:
  7.2 109.6 %copy-start = (bf16[2560,640]{1,0:T(8,128)(2,1)S(1)}, bf16[2560,640]{1,0:T(8,128)(2,1)}, u32[]{:S(2)}) copy-start(bf16[2560,640]{1,0:T(8,128)(2,1)} %param.6) | copy-start | bytes 9830404
  7.2 115.3 %all-gather.2.cloned.1.call-start = ((), (), s32[]{:S(2)}) async-start(), calls=%async_computation.2 | async-start | bytes 6553600 | tf_op jit(solution)/shard_map/all_gather | solution.py:25
  7.9 234.3 %all-reduce.3.cloned.1.call-start = ((), (), s32[]{:S(2)}) async-start(), calls=%async_computation.4 | async-start | bytes 10485760 | tf_op jit(solution)/shard_map/psum | solution.py:31
  114.4 2.4 copy-start.2
  131.8 296.4 %reduce-scatter.2.cloned.1.call-start = ((), (), s32[]{:S(2)}) async-start(), calls=%async_computation.3 | async-start | bytes 10813440 | tf_op jit(solution)/shard_map/reduce_scatter | solution.py:39
  245.3 1.1 copy-start.3
  253.3 1.3 copy-start.4
  271.6 158.2 %copy-start.1 = (bf16[2560,640]{1,0:T(8,128)(2,1)S(1)}, bf16[2560,640]{1,0:T(8,128)(2,1)}, u32[]{:S(2)}) copy-start(bf16[2560,640]{1,0:T(8,128)(2,1)} %param.6) | copy-start | bytes 9830404
Sparse Core Ops, SparseCore 0:
  9.6 99.4 all-gather.1
  131.9 110.3 all-reduce.2
  253.4 174.6 reduce-scatter.1
